TPU v7x, 512 devices: a whole 4x8x8 slice. The times are simulated.
512 devices in a mesh: pipe: 8 (over y_hi, core), ctx: 16 (over z, y_lo), dp: 4 (over x).
Axes of the slice: x: 4, y: 8 (y_hi: 4, y_lo: 2; y = y_hi * 2 + y_lo), z: 8, core: 2. Of those that a mesh axis runs over, the one named last changes fastest.
Arguments:
- state: bfloat16 [8, 4, 2048, 1024], P('pipe', 'dp', 'ctx'), may hold values from -36 to 36
- weights: bfloat16 [2, 8, 1024, 256], P(None, 'pipe'), may hold values from -0.1875 to 0.1875
- out_grad: bfloat16 [2, 8, 4, 2048, 1024], P(None, 'pipe', 'dp', 'ctx'), may hold values from -0.59765625 to 0.59765625
- start_span: int32 [8, 4], P(None, 'dp'), may hold values from 0 to 1
- block_order: int32 [32], replicated, may hold values from 0 to 31, each once
Outputs:
- state_out: bfloat16 [8, 4, 2048, 1024], P('pipe', 'dp', 'ctx')
- weight_grads: float32 [2, 8, 1024, 256], P(None, 'pipe')
All inputs are finite; a program needn't handle non-finite values.
Results may differ from a plain program's by a relative error of at most 0.012.
Values may be sent and summed in bfloat16 or wider, within the bound.
No kernel may reach another device: no remote copies, remote signals or barrier semaphores. Data moves between devices by JAX's collectives and lax.ppermute only.
A program may use at most 64 MiB of HBM per device.

v0:
```python
import math

import jax
import jax.numpy as jnp
from jax import lax
from jax.sharding import PartitionSpec as P

EPS = 1e-05


def from_behind(block, axis, distance):
    devices = range(lax.axis_size(axis))
    route = [((i - distance) % len(devices), i) for i in devices]
    return lax.ppermute(block, axis, route)


def rms_scale(values):
    return lax.rsqrt(jnp.mean(values * values, axis=-1, keepdims=True) + EPS)


def token_positions(block_order, seq_total):
    half_count = block_order.shape[0]
    half_len = seq_total // half_count
    row_ids = jnp.arange(seq_total, dtype=jnp.int32)
    selected = (row_ids // half_len)[:, None] == jnp.arange(half_count, dtype=jnp.int32)[None, :]
    block_ids = jnp.sum(jnp.where(selected, block_order[None, :], 0), axis=1)
    return block_ids * half_len + row_ids % half_len


def shards(state, weights, out_grad, start_span, block_order):
    tok_rows = state.shape[2]
    feat_width = state.shape[3]
    head_dim = weights.shape[3] // 2
    head_count = feat_width // head_dim
    group_size = math.gcd(head_count, 4)
    group_count = head_count // group_size
    span_count = weights.shape[0]
    section_count = lax.axis_size("pipe")
    seq_total = tok_rows * lax.axis_size("ctx")
    score_scale = 1.0 / math.sqrt(head_dim)
    all_positions = token_positions(block_order, seq_total)
    own_positions = lax.dynamic_slice_in_dim(
        all_positions, lax.axis_index("ctx") * tok_rows, tok_rows
    )
    causal = all_positions[None, :] <= own_positions[:, None]
    section_index = lax.axis_index("pipe")
    carried = state[0, 0]
    start_column = start_span[:, 0]
    weight_grads = jnp.zeros((span_count, feat_width, 2 * head_dim), jnp.float32)
    for tick_index in range(out_grad.shape[0]):
        anchor = (section_index - tick_index) % section_count
        first_span = jnp.sum(
            jnp.where(jnp.arange(section_count, dtype=jnp.int32) == anchor, start_column, 0)
        )
        span_index = (first_span + (anchor + tick_index) // section_count) % 2
        weight = lax.dynamic_index_in_dim(weights[:, 0], span_index, 0, keepdims=False)
        widened = carried.astype(jnp.float32)
        normed = (widened * rms_scale(widened)).astype(jnp.bfloat16)
        split_heads = widened.reshape(tok_rows, head_count, head_dim)
        queries = (split_heads * rms_scale(split_heads)).astype(jnp.bfloat16)
        projected = jnp.dot(normed, weight, preferred_element_type=jnp.float32)
        key_raw = projected[:, :head_dim]
        key_scale = rms_scale(key_raw)
        key_unit = key_raw * key_scale
        own_rows = jnp.concatenate([key_unit, projected[:, head_dim:]], axis=1).astype(jnp.bfloat16)
        gathered = lax.all_gather(own_rows, "ctx", axis=0, tiled=True)
        key_rows = gathered[:, :head_dim]
        value_rows = gathered[:, head_dim:]
        query_groups = queries.reshape(tok_rows, group_count, group_size, head_dim).transpose(
            1, 0, 2, 3
        )

        def forward_group(query_part):
            scores = (
                jnp.einsum("qhd,kd->hqk", query_part, key_rows, preferred_element_type=jnp.float32)
                * score_scale
            )
            exponent = jnp.where(causal[None], jnp.exp(scores), 0.0)
            total_weight = jnp.sum(exponent, axis=-1, keepdims=True)
            probs = (exponent / total_weight).astype(jnp.bfloat16)
            attended = jnp.einsum(
                "hqk,kd->qhd", probs, value_rows, preferred_element_type=jnp.float32
            )
            return (probs, attended)

        probs, attended = lax.map(forward_group, query_groups)
        output = attended.transpose(1, 0, 2, 3).reshape(tok_rows, feat_width)
        updated = (widened + output * rms_scale(output)).astype(jnp.bfloat16)
        carried = from_behind(updated, "pipe", 1)
        upstream = out_grad[tick_index, 0, 0]
        upstream_groups = upstream.reshape(tok_rows, group_count, group_size, head_dim).transpose(
            1, 0, 2, 3
        )
        row_delta = jnp.sum(upstream_groups.astype(jnp.float32) * attended, axis=-1).transpose(
            0, 2, 1
        )
        key_grad = jnp.zeros((tok_rows * lax.axis_size("ctx"), head_dim), jnp.float32)
        value_grad = jnp.zeros((tok_rows * lax.axis_size("ctx"), head_dim), jnp.float32)
        for head_block in range(group_count):
            prob_part = probs[head_block]
            value_grad = value_grad + jnp.einsum(
                "hqk,qhd->kd",
                prob_part,
                upstream_groups[head_block],
                preferred_element_type=jnp.float32,
            )
            prob_grad = jnp.einsum(
                "qhd,kd->hqk",
                upstream_groups[head_block],
                value_rows,
                preferred_element_type=jnp.float32,
            )
            score_grad = (
                prob_part.astype(jnp.float32)
                * (prob_grad - row_delta[head_block][..., None])
                * score_scale
            ).astype(jnp.bfloat16)
            key_grad = key_grad + jnp.einsum(
                "hqk,qhd->kd",
                score_grad,
                query_groups[head_block],
                preferred_element_type=jnp.float32,
            )
        key_sums = lax.psum_scatter(
            jnp.concatenate([key_grad, value_grad], axis=1).astype(jnp.bfloat16),
            "ctx",
            scatter_dimension=0,
            tiled=True,
        ).astype(jnp.float32)
        key_delta = key_sums[:, :head_dim]
        key_back = key_scale * (
            key_delta - key_unit * jnp.mean(key_delta * key_unit, axis=-1, keepdims=True)
        )
        grad_rows = jnp.concatenate([key_back, key_sums[:, head_dim:]], axis=1).astype(jnp.bfloat16)
        local_grad = lax.dot_general(
            normed, grad_rows, (((0,), (0,)), ((), ())), preferred_element_type=jnp.float32
        )
        span_mask = (jnp.arange(span_count, dtype=jnp.int32) == span_index).astype(jnp.float32)[
            :, None, None
        ]
        masked_grad = span_mask * local_grad
        weight_grads = weight_grads + masked_grad
    weight_grads = lax.psum(weight_grads, ("ctx", "dp"))
    return (carried[None, None], weight_grads[:, None])


def solution(mesh):
    return jax.shard_map(
        shards,
        mesh=mesh,
        in_specs=(
            P("pipe", "dp", "ctx", None),
            P(None, "pipe", None, None),
            P(None, "pipe", "dp", "ctx", None),
            P(None, "dp"),
            P(),
        ),
        out_specs=(P("pipe", "dp", "ctx", None), P(None, "pipe", None, None)),
        check_vma=False,
    )
```

profile of v0, /device:TPU:16, one launch (start us, length us, event | category | flops | bytes accessed | tf_op | source)
XLA Modules:
  0.0 990.2 jit_solution(8186478735265335391)
XLA Ops:
  16.2 74.4 %all-gather.3.cloned.1.call-done = bf16[2048,256]{1,0:T(8,128)(2,1)} async-done(((bf16[128,256]{1,0:T(8,128)(2,1)}), bf16[2048,256]{1,0:T(8,128)(2,1)}) %all-gather.3.cloned.1.call-update) | async-done | bytes 1048592 | tf_op jit(solution)/shard_map/all_gather | solution.py:66
  92.7 2.5 broadcast.232.clone2
  95.2 22.0 %while.26 = (s32[]{:T(128)}, bf16[2,4,128,2048]{2,3,1,0:T(8,128)(2,1)}, f32[2,128,4,128]{3,1,2,0:T(8,128)}, bf16[2,128,4,128]{1,3,2,0:T(8,128)(2,1)}, bf16[2048,...) while((s32[]{:T(128)}, ...), condition=%wide.region_7.8_spmd.clone, body=%wide.region_5.7_spmd.clone.sunk | while | flops 548666880 | bytes 33962720 | solution.py:86
  100.5 2.5 copy.225
  103.0 3.2 constant_dynamic-update-slice_fusion.4
  111.5 2.5 copy.225
  114.0 3.1 constant_dynamic-update-slice_fusion.4
  122.8 6.8 collective-permute-done
  139.0 4.0 convolution_bitcast_fusion.8
  143.1 3.4 fusion.39
  149.1 56.5 %all-gather.5.cloned.1.call-done = bf16[2048,256]{1,0:T(8,128)(2,1)} async-done(((bf16[128,256]{1,0:T(8,128)(2,1)}), bf16[2048,256]{1,0:T(8,128)(2,1)}) %all-gather.5.cloned.1.call-update) | async-done | bytes 1048592 | tf_op jit(solution)/shard_map/all_gather | solution.py:66
  207.7 2.5 broadcast.232.clone
  210.1 22.0 %while.27 = (s32[]{:T(128)}, bf16[2,4,128,2048]{2,3,1,0:T(8,128)(2,1)}, f32[2,128,4,128]{3,1,2,0:T(8,128)}, bf16[2,128,4,128]{1,3,2,0:T(8,128)(2,1)}, bf16[2048,...) while((s32[]{:T(128)}, ...), condition=%wide.region_15.16_spmd.clone, body=%wide.region_13.15_spmd.clone.sunk | while | flops 548666880 | bytes 33962720 | solution.py:86
  215.5 2.5 copy.226
  218.0 3.2 constant_dynamic-update-slice_fusion.5
  226.5 2.5 copy.226
  229.0 3.1 constant_dynamic-update-slice_fusion.5
  238.2 3.9 convolution_bitcast_fusion.4
  242.1 4.0 fusion.37
  248.4 35.8 %reduce-scatter.3.cloned.1.call-done = bf16[128,256]{1,0:T(8,128)(2,1)} async-done(((bf16[2048,256]{1,0:T(8,128)(2,1)}), bf16[128,256]{1,0:T(8,128)(2,1)}) %reduce-scatter.3.cloned.1.call-update) | async-done | bytes 65552 | tf_op jit(solution)/shard_map/reduce_scatter | solution.py:124
  287.2 73.8 %reduce-scatter.5.cloned.1.call-done = bf16[128,256]{1,0:T(8,128)(2,1)} async-done(((bf16[2048,256]{1,0:T(8,128)(2,1)}), bf16[128,256]{1,0:T(8,128)(2,1)}) %reduce-scatter.5.cloned.1.call-update) | async-done | bytes 65552 | tf_op jit(solution)/shard_map/reduce_scatter | solution.py:124
  370.5 7.2 collective-permute-done.1
  377.7 602.2 %all-reduce.2.cloned.1.call-done = f32[2,1,1024,256]{3,2,1,0:T(8,128)} async-done(((f32[2,1,1024,256]{3,2,1,0:T(8,128)}), f32[2,1,1024,256]{3,2,1,0:T(8,128)}) %all-reduce.2.cloned.1.call-update) | async-done | bytes 2097168 | tf_op jit(solution)/shard_map/psum | solution.py:143
  980.6 3.0 copy.256
  (168 shorter events, 71.8 us)
Async XLA Ops:
  7.2 3.3 copy-start
  7.2 8.0 copy-start.23
  7.2 83.4 %all-gather.3.cloned.1.call-start = ((), (), s32[]{:S(2)}) async-start(), calls=%async_computation.2 | async-start | bytes 1114112 | tf_op jit(solution)/shard_map/all_gather | solution.py:66
  12.6 192.9 %all-gather.5.cloned.1.call-start = ((), (), s32[]{:S(2)}) async-start(), calls=%async_computation.3 | async-start | bytes 1114112 | tf_op jit(solution)/shard_map/all_gather | solution.py:66
  95.2 24.8 %copy-start.1 = (bf16[1,1,128,1024]{3,2,1,0:T(8,128)(2,1)S(1)}, bf16[1,1,128,1024]{3,2,1,0:T(8,128)(2,1)}, u32[]{:S(2)}) copy-start(bf16[1,1,128,1024]{3,2,1,0:T(8,128)(2,1)} %param.9) | copy-start | bytes 786436
  103.0 3.2 copy-start.14
  103.0 3.2 copy-start.16
  117.1 14.0 %copy-start.8 = (bf16[2,1,1,128,1024]{4,3,2,1,0:T(8,128)(2,1)S(1)}, bf16[2,1,1,128,1024]{4,3,2,1,0:T(8,128)(2,1)}, u32[]{:S(2)}) copy-start(bf16[2,1,1,128,1024]{4,3,2,1,0:T(8,128)(2,1)} %param.11) | copy-start | bytes 1572868
  120.1 9.4 collective-permute-start
  129.6 18.6 %copy-start.2 = (bf16[128,1024]{1,0:T(8,128)(2,1)}, bf16[128,1024]{1,0:T(8,128)(2,1)S(1)}, u32[]{:S(2)}) copy-start(bf16[128,1024]{1,0:T(8,128)(2,1)S(1)} %collective-permute-done) | copy-start | bytes 786436
  130.0 4.4 copy-start.5
  131.1 153.1 %reduce-scatter.3.cloned.1.call-start = ((), (), s32[]{:S(2)}) async-start(), calls=%async_computation.4 | async-start | bytes 1114112 | tf_op jit(solution)/shard_map/reduce_scatter | solution.py:124
  147.6 213.4 %reduce-scatter.5.cloned.1.call-start = ((), (), s32[]{:S(2)}) async-start(), calls=%async_computation.5 | async-start | bytes 1114112 | tf_op jit(solution)/shard_map/reduce_scatter | solution.py:124
  218.0 3.2 copy-start.10
  218.0 3.2 copy-start.12
  232.1 3.8 copy-start.4
  232.1 6.1 copy-start.7
  242.1 44.6 %copy-start.20 = (f32[128]{0:T(128)S(1)}, f32[128]{0:T(128)}, u32[]{:S(2)}) copy-start(f32[128]{0:T(128)} %copy-done.19) | copy-start | bytes 1540
  246.1 114.8 %copy-start.6 = (f32[128,256]{1,0:T(8,128)S(1)}, f32[128,256]{1,0:T(8,128)}, u32[]{:S(2)}) copy-start(f32[128,256]{1,0:T(8,128)} %copy-done.5) | copy-start | bytes 393220
  246.1 114.8 %copy-start.18 = (f32[128]{0:T(128)S(1)}, f32[128]{0:T(128)}, u32[]{:S(2)}) copy-start(f32[128]{0:T(128)} %copy-done.17) | copy-start | bytes 1540
  246.1 117.4 %copy-start.3 = (bf16[128,1024]{1,0:T(8,128)(2,1)S(1)}, bf16[128,1024]{1,0:T(8,128)(2,1)}, u32[]{:S(2)}) copy-start(bf16[128,1024]{1,0:T(8,128)(2,1)} %copy-done.2) | copy-start | bytes 786436
  246.1 117.4 %copy-start.22 = (f32[128]{0:T(128)S(1)}, f32[128]{0:T(128)}, u32[]{:S(2)}) copy-start(f32[128]{0:T(128)} %copy-done.21) | copy-start | bytes 1540
  248.4 731.6 %all-reduce.2.cloned.1.call-start = ((), (), s32[]{:S(2)}) async-start(), calls=%async_computation.6 | async-start | bytes 4194304 | tf_op jit(solution)/shard_map/psum | solution.py:143
  368.5 9.2 collective-permute-start.1
  (15 other events, 35.9 us)
Sparse Core Ops, SparseCore 0:
  12.8 77.7 all-gather.2
  131.2 74.3 all-gather.4
  208.4 75.7 reduce-scatter.2
  287.7 73.2 reduce-scatter.4
  365.7 614.1 all-reduce.1
where the time goes:
time: 992 us; the launch traced here: 990 us
  waiting for transfers between devices  857 us (86%)
  local copies, waits for them, and re-layouts  44.1 us (4%)
  matrix products  43.5 us (4%)
  other arithmetic  25.8 us (3%)
  between operations  15.7 us (2%)
    psum x1, waiting for transfers between devices, shards(): weight_grads = lax.psum(weight_grads, ('ctx', 'dp'))  602 us
    all_gather x2, waiting for transfers between devices, shards(): gathered = lax.all_gather(own_rows, 'ctx', axis=0, tiled=True)  131 us
    reduce_scatter x2, waiting for transfers between devices, shards(): lax.psum_scatter(jnp.concatenate([key_grad, value_grad], axis=1).astype(j...  110 us
    dynamic_update_slice x8, local copies, waits for them, and re-layouts, shards(): probs, attended = lax.map(forward_group, query_groups)  22.5 us
  transfers between devices with their start and end apart: 7, of which 7 were waited for; matrix products, arithmetic and copies ran while one was open for 7% of the time, Pallas kernels for 0%

commit v1 on v0

v1 whole, which is shorter than its diff:
```python
import math

import jax
import jax.numpy as jnp
from jax import lax
from jax.sharding import PartitionSpec as P

EPS = 1e-05


def from_behind(block, axis, distance):
    devices = range(lax.axis_size(axis))
    route = [((i - distance) % len(devices), i) for i in devices]
    return lax.ppermute(block, axis, route)


def rms_scale(values):
    return lax.rsqrt(jnp.mean(values * values, axis=-1, keepdims=True) + EPS)


def token_positions(block_order, seq_total):
    half_count = block_order.shape[0]
    half_len = seq_total // half_count
    row_ids = jnp.arange(seq_total, dtype=jnp.int32)
    selected = (row_ids // half_len)[:, None] == jnp.arange(half_count, dtype=jnp.int32)[None, :]
    block_ids = jnp.sum(jnp.where(selected, block_order[None, :], 0), axis=1)
    return block_ids * half_len + row_ids % half_len


def swap(blocks, axes):
    return lax.all_to_all(blocks, axes, 0, 0, tiled=True)


def repeat_rows(rows, count):
    return jnp.broadcast_to(rows[None], (count,) + rows.shape)


def project(carried, weight):
    tok_rows, feat_width = carried.shape
    head_dim = weight.shape[1] // 2
    widened = carried.astype(jnp.float32)
    normed = (widened * rms_scale(widened)).astype(jnp.bfloat16)
    split_heads = widened.reshape(tok_rows, feat_width // head_dim, head_dim)
    queries = (split_heads * rms_scale(split_heads)).astype(jnp.bfloat16)
    projected = jnp.dot(normed, weight, preferred_element_type=jnp.float32)
    key_raw = projected[:, :head_dim]
    key_scale = rms_scale(key_raw)
    key_unit = key_raw * key_scale
    own_rows = jnp.concatenate([key_unit, projected[:, head_dim:]], axis=1).astype(jnp.bfloat16)
    return widened, normed, queries, key_scale, key_unit, own_rows


def forward(widened, queries, key_rows, value_rows, causal, score_scale):
    tok_rows, feat_width = widened.shape
    scores = (
        jnp.einsum("qhd,kd->hqk", queries, key_rows, preferred_element_type=jnp.float32)
        * score_scale
    )
    exponent = jnp.where(causal[None], jnp.exp(scores), 0.0)
    total_weight = jnp.sum(exponent, axis=-1, keepdims=True)
    probs = (exponent / total_weight).astype(jnp.bfloat16)
    attended = jnp.einsum("hqk,kd->qhd", probs, value_rows, preferred_element_type=jnp.float32)
    output = attended.reshape(tok_rows, feat_width)
    updated = (widened + output * rms_scale(output)).astype(jnp.bfloat16)
    return probs, attended, updated


def backward(probs, attended, queries, value_rows, upstream, score_scale):
    upstream = upstream.reshape(queries.shape)
    row_delta = jnp.sum(upstream.astype(jnp.float32) * attended, axis=-1).transpose(1, 0)
    value_grad = jnp.einsum("hqk,qhd->kd", probs, upstream, preferred_element_type=jnp.float32)
    prob_grad = jnp.einsum("qhd,kd->hqk", upstream, value_rows, preferred_element_type=jnp.float32)
    score_grad = (
        probs.astype(jnp.float32) * (prob_grad - row_delta[..., None]) * score_scale
    ).astype(jnp.bfloat16)
    key_grad = jnp.einsum("hqk,qhd->kd", score_grad, queries, preferred_element_type=jnp.float32)
    return jnp.concatenate([key_grad, value_grad], axis=1).astype(jnp.bfloat16)


def finish(received, normed, key_scale, key_unit):
    head_dim = key_unit.shape[1]
    key_sums = jnp.sum(received.astype(jnp.float32), axis=0)
    key_delta = key_sums[:, :head_dim]
    key_back = key_scale * (
        key_delta - key_unit * jnp.mean(key_delta * key_unit, axis=-1, keepdims=True)
    )
    grad_rows = jnp.concatenate([key_back, key_sums[:, head_dim:]], axis=1).astype(jnp.bfloat16)
    return lax.dot_general(
        normed, grad_rows, (((0,), (0,)), ((), ())), preferred_element_type=jnp.float32
    )


def shards(state, weights, out_grad, start_span, block_order):
    tok_rows = state.shape[2]
    feat_width = state.shape[3]
    head_dim = weights.shape[3] // 2
    span_count = weights.shape[0]
    section_count = lax.axis_size("pipe")
    ctx_count = lax.axis_size("ctx")
    all_count = ctx_count * lax.axis_size("dp")
    seq_total = tok_rows * ctx_count
    score_scale = 1.0 / math.sqrt(head_dim)
    all_positions = token_positions(block_order, seq_total)
    own_positions = lax.dynamic_slice_in_dim(
        all_positions, lax.axis_index("ctx") * tok_rows, tok_rows
    )
    causal = all_positions[None, :] <= own_positions[:, None]
    section_index = lax.axis_index("pipe")
    start_column = start_span[:, 0]

    def span_at(tick_index):
        anchor = (section_index - tick_index) % section_count
        first_span = jnp.sum(
            jnp.where(jnp.arange(section_count, dtype=jnp.int32) == anchor, start_column, 0)
        )
        return (first_span + (anchor + tick_index) // section_count) % 2

    tick_count = out_grad.shape[0]
    carried = state[0, 0]
    waiting = None
    weight_grads = jnp.zeros((span_count, feat_width, 2 * head_dim), jnp.float32)

    def add_grads(weight_grads, received, normed, key_scale, key_unit, span_index):
        local_grad = finish(received, normed, key_scale, key_unit)
        used = jnp.arange(span_count, dtype=jnp.int32) == span_index
        return weight_grads + jnp.where(used[:, None, None], local_grad[None], 0.0)

    for tick_index in range(tick_count):
        span_index = span_at(tick_index)
        weight = lax.dynamic_index_in_dim(weights[:, 0], span_index, 0, keepdims=False)
        widened, normed, queries, key_scale, key_unit, own_rows = project(carried, weight)
        outgoing = repeat_rows(own_rows, ctx_count)
        if waiting is None:
            gathered = swap(outgoing, "ctx")
        else:
            both = swap(jnp.concatenate([outgoing, waiting[0]], axis=1), "ctx")
            gathered = both[:, :tok_rows]
            weight_grads = add_grads(weight_grads, both[:, tok_rows:], *waiting[1])
        gathered = gathered.reshape(seq_total, 2 * head_dim)
        key_rows = gathered[:, :head_dim]
        value_rows = gathered[:, head_dim:]
        probs, attended, updated = forward(
            widened, queries, key_rows, value_rows, causal, score_scale
        )
        carried = from_behind(updated, "pipe", 1)
        terms = backward(
            probs, attended, queries, value_rows, out_grad[tick_index, 0, 0], score_scale
        )
        waiting = (
            terms.reshape(ctx_count, tok_rows, 2 * head_dim),
            (normed, key_scale, key_unit, span_index),
        )
    weight_grads = add_grads(weight_grads, swap(waiting[0], "ctx"), *waiting[1])
    part_rows = feat_width // all_count
    parts = (
        weight_grads.astype(jnp.bfloat16)
        .reshape(span_count, all_count, part_rows, 2 * head_dim)
        .transpose(1, 0, 2, 3)
    )
    everyone = ("ctx", "dp")
    summed = jnp.sum(swap(parts, everyone).astype(jnp.float32), axis=0).astype(jnp.bfloat16)
    whole = swap(repeat_rows(summed, all_count), everyone)
    weight_grads = (
        whole.transpose(1, 0, 2, 3)
        .reshape(span_count, feat_width, 2 * head_dim)
        .astype(jnp.float32)
    )
    return (carried[None, None], weight_grads[:, None])


def solution(mesh):
    return jax.shard_map(
        shards,
        mesh=mesh,
        in_specs=(
            P("pipe", "dp", "ctx", None),
            P(None, "pipe", None, None),
            P(None, "pipe", "dp", "ctx", None),
            P(None, "dp"),
            P(),
        ),
        out_specs=(P("pipe", "dp", "ctx", None), P(None, "pipe", None, None)),
        check_vma=False,
    )
```

time: 992 us -> 251 us (0.25)
  waiting for transfers between devices: 857 us -> 124 us
  blocking collectives: 0 us -> 36 us
  local copies, waits for them, and re-layouts: 44.1 us -> 12.7 us
  starting transfers between devices: 4.23 us -> 32.1 us
  matrix products: 43.5 us -> 24.3 us
  between operations: 15.7 us -> 2.59 us
    psum x1 -> x0, waiting for transfers between devices: 602 us -> none  [shards(): weight_grads = lax.psum(weight_grads, ('ctx', 'dp'))]
    all_gather x2 -> x0, waiting for transfers between devices: 131 us -> none  [shards(): gathered = lax.all_gather(own_rows, 'ctx', axis=0, tiled=True)]
    reduce_scatter x2 -> x0, waiting for transfers between devices: 110 us -> none  [shards(): lax.psum_scatter(jnp.concatenate([key_grad, value_grad], axis=1).astype(j...]
    all_to_all x0 -> x4, waiting for transfers between devices: none -> 109 us  [swap(): return lax.all_to_all(blocks, axes, 0, 0, tiled=True)]
    all_to_all x0 -> x1, blocking collectives: none -> 36 us  [swap(): return lax.all_to_all(blocks, axes, 0, 0, tiled=True)]
    all_to_all x0 -> x4, starting transfers between devices: none -> 28.3 us  [swap(): return lax.all_to_all(blocks, axes, 0, 0, tiled=True)]
    dynamic_update_slice x8 -> x0, local copies, waits for them, and re-layouts: 22.5 us -> none  [shards(): probs, attended = lax.map(forward_group, query_groups)]
    dot_general x20 -> x14, matrix products: 43.5 us -> 24.3 us  [the longest x2 6.52 us: forward(): jnp.einsum('hqk,kd->qhd', probs, value_rows, preferred_element_type=jnp.f...]
  transfers between devices with their start and end apart: 7 -> 6, of which waited for: 7 -> 6; matrix products, arithmetic and copies ran while one was open for 7% -> 6% of each run, Pallas kernels for 0% -> 0%
where the time goes in v1:
time: 251 us; the launch traced here: 250 us
  waiting for transfers between devices  124 us (49%)
  blocking collectives  36 us (14%)
  starting transfers between devices  32.1 us (13%)
  matrix products  24.3 us (10%)
  other arithmetic  18.8 us (7%)
  local copies, waits for them, and re-layouts  12.7 us (5%)
  between operations  2.59 us (1%)
    all_to_all x4, waiting for transfers between devices, swap(): return lax.all_to_all(blocks, axes, 0, 0, tiled=True)  109 us
    all_to_all x1, blocking collectives, swap(): return lax.all_to_all(blocks, axes, 0, 0, tiled=True)  36 us
    all_to_all x4, starting transfers between devices, swap(): return lax.all_to_all(blocks, axes, 0, 0, tiled=True)  28.3 us
    ppermute x2, waiting for transfers between devices, from_behind(): return lax.ppermute(block, axis, route)  14.9 us
    dot_general x2, matrix products, forward(): jnp.einsum('hqk,kd->qhd', probs, value_rows, preferred_element_type=jnp.f...  6.52 us
    dot_general x2, matrix products, forward(): jnp.einsum('qhd,kd->hqk', queries, key_rows, preferred_element_type=jnp.f...  5.68 us
  transfers between devices with their start and end apart: 6, of which 6 were waited for; matrix products, arithmetic and copies ran while one was open for 6% of the time, Pallas kernels for 0%

profile of v1, /device:TPU:16, one launch (start us, length us, event | category | flops | bytes accessed | tf_op | source)
XLA Modules:
  0.0 250.3 jit_solution(15148124485568726557)
XLA Ops:
  5.6 11.5 %all-to-all-start = ((bf16[16,128,256]{2,1,0:T(8,128)(2,1)}), bf16[16,128,256]{2,1,0:T(8,128)(2,1)}, u32[]{:S(2)}, u32[]{:S(2)}) async-start(bf16[16,128,256]{2,1,0:T(8,128)(2,1)} %broadcast_in_dim.118), calls=%async_computation | async-start | bytes 2097152 | tf_op jit(solution)/shard_map/all_to_all | solution.py:31
  17.8 1.8 fusion.67
  21.4 23.5 %all-to-all-done = bf16[16,128,256]{2,1,0:T(8,128)(2,1)} async-done(((bf16[16,128,256]{2,1,0:T(8,128)(2,1)}), bf16[16,128,256]{2,1,0:T(8,128)(2,1)}, u32[]{:S(2)}, u32[]{:S(2)}) %all-to-all-start) | async-done | bytes 1048608 | tf_op jit(solution)/shard_map/all_to_all | solution.py:31
  44.9 2.8 %fusion.8 = (f32[8,128]{1,0:T(8,128)S(1)}, f32[2048,128,8]{1,0,2:T(8,128)S(1)}) fusion(pred[128,2048]{0,1:T(8,128)(4,1)S(1)} %broadcast_compare_fusion.1, f32[128,8,128]{0,2,1:T(8,128)S(1)} %get-tuple-element.17, f32[128,8]{0,1:T(8,128)S(1)} %add_rsqrt_fusion.1, bf16[2048,256]{1,0:T(8,128)(2,1)} %bitcast.4), kind=kOutput, calls=%fused_computation.18 | convolution fusion | flops 543423488 | bytes 9707520 | tf_op jit(solution)/shard_map/qhd,kd->hqk/dot_general | solution.py:56
  47.7 3.1 %fusion.27 = (f32[128]{0:T(128)S(1)}, f32[128,8]{0,1:T(8,128)S(1)}, f32[128,8,128]{2,0,1:T(8,128)S(1)}) fusion(bf16[128,8,128]{0,2,1:T(8,128)(2,1)S(1)} %bitcast.195, f32[2048,128,8]{1,0,2:T(8,128)S(1)} %get-tuple-element.23, f32[8,128]{1,0:T(8,128)S(1)} %get-tuple-element.22, pred[128,2048]{0,1:T(8,128)(4,1)S(1)} %broadcast_compare_fusion.1, ...), kind=kOutput, calls=%fused_computation.57 | convolution fusion | flops 545913728 | bytes 9970176 | tf_op jit(solution)/shard_map/hqk,kd->qhd/dot_general | solution.py:62
  50.9 1.8 fusion.7
  53.5 1.9 collective-permute-start
  55.4 2.6 %fusion.6 = bf16[2048,8,128]{2,0,1:T(8,128)(2,1)S(1)} fusion(bf16[2048,8,128]{2,0,1:T(8,128)(2,1)S(1)} %fusion.7, bf16[128,8,128]{0,2,1:T(8,128)(2,1)S(1)} %bitcast.196, f32[8,128]{1,0:T(8,128)S(1)} %bitcast.207, bf16[2048,256]{1,0:T(8,128)(2,1)} %bitcast.4), kind=kOutput, calls=%fused_computation.10 | convolution fusion | flops 547356672 | bytes 9179136 | tf_op jit(solution)/shard_map/qhd,kd->hqk/dot_general | solution.py:72
  63.7 1.6 maximum_maximum_fusion
  65.3 6.6 %all-to-all-start.1 = ((bf16[16,256,256]{1,2,0:T(8,128)(2,1)}), bf16[16,256,256]{1,2,0:T(8,128)(2,1)S(1)}, u32[]{:S(2)}, u32[]{:S(2)}) async-start(bf16[16,256,256]{1,2,0:T(8,128)(2,1)} %maximum_maximum_fusion), calls=%async_computation.1 | async-start | bytes 4194304 | tf_op jit(solution)/shard_map/all_to_all | solution.py:31
  71.9 1.8 copy.99
  73.8 49.0 %all-to-all-done.1 = bf16[16,256,256]{1,2,0:T(8,128)(2,1)S(1)} async-done(((bf16[16,256,256]{1,2,0:T(8,128)(2,1)}), bf16[16,256,256]{1,2,0:T(8,128)(2,1)S(1)}, u32[]{:S(2)}, u32[]{:S(2)}) %all-to-all-start.1) | async-done | bytes 2097184 | tf_op jit(solution)/shard_map/all_to_all | solution.py:31
  123.9 2.3 copy.93
  126.2 2.9 %fusion.9 = (f32[8,128]{1,0:T(8,128)S(1)}, f32[2048,128,8]{1,0,2:T(8,128)S(1)}) fusion(pred[128,2048]{0,1:T(8,128)(4,1)} %copy-done.7, f32[128,8]{0,1:T(8,128)S(1)} %add_rsqrt_fusion, bf16[2048,256]{1,0:T(8,128)(2,1)} %bitcast.201, bf16[128,8,128]{0,2,1:T(8,128)(2,1)S(1)} %bitcast.189), kind=kOutput, calls=%fused_computation.19 | convolution fusion | flops 543554560 | bytes 9445376 | tf_op jit(solution)/shard_map/qhd,kd->hqk/dot_general | solution.py:56
  129.2 1.8 fusion.3
  131.0 3.4 %fusion.22 = (f32[128,8]{0,1:T(8,128)S(1)}, f32[128]{0:T(128)}, f32[128,8,128]{2,0,1:T(8,128)}) fusion(bf16[128,8,128]{0,2,1:T(8,128)(2,1)S(1)} %bitcast.198, f32[2048,128,8]{1,0,2:T(8,128)S(1)} %get-tuple-element.26, f32[8,128]{1,0:T(8,128)S(1)} %get-tuple-element.25, pred[128,2048]{0,1:T(8,128)(4,1)S(1)} %copy-done.8, bf16[2048,256]{1,0:T(8,128)(2,1)S(1)} %bitcast.202), kind=kOutput, calls=%fused_computation.50 | convolution fusion | flops 545913728 | bytes 9970176 | tf_op jit(solution)/shard_map/hqk,kd->qhd/dot_general | solution.py:62
  140.0 4.3 %all-to-all-start.2 = ((bf16[16,128,256]{1,2,0:T(8,128)(2,1)}), bf16[16,128,256]{1,2,0:T(8,128)(2,1)}, u32[]{:S(2)}, u32[]{:S(2)}) async-start(bf16[16,128,256]{1,2,0:T(8,128)(2,1)} %pad_maximum_fusion), calls=%async_computation.2 | async-start | bytes 2097152 | tf_op jit(solution)/shard_map/all_to_all | solution.py:31
  146.8 24.6 %all-to-all-done.2 = bf16[16,128,256]{1,2,0:T(8,128)(2,1)} async-done(((bf16[16,128,256]{1,2,0:T(8,128)(2,1)}), bf16[16,128,256]{1,2,0:T(8,128)(2,1)}, u32[]{:S(2)}, u32[]{:S(2)}) %all-to-all-start.2) | async-done | bytes 1048608 | tf_op jit(solution)/shard_map/all_to_all | solution.py:31
  176.5 36.0 %all_to_all.25 = bf16[64,2,16,256]{3,2,1,0:T(8,128)(2,1)S(1)} all-to-all(bf16[64,2,16,256]{3,2,1,0:T(8,128)(2,1)S(1)} %add_convert_fusion), channel_id=1, replica_groups=mesh['pipe'=8,'ctx'=16,'dp'=4] {'ctx','dp'}, dimensions={0} | all-to-all | bytes 2097152 | tf_op jit(solution)/shard_map/all_to_all | solution.py:31
  213.7 5.9 %all-to-all-start.4 = ((bf16[64,2,16,256]{3,2,1,0:T(8,128)(2,1)}), bf16[64,2,16,256]{3,2,1,0:T(8,128)(2,1)S(1)}, u32[]{:S(2)}, u32[]{:S(2)}) async-start(bf16[64,2,16,256]{3,2,1,0:T(8,128)(2,1)} %broadcast_in_dim.133), calls=%async_computation.4 | async-start | bytes 2097152 | tf_op jit(solution)/shard_map/all_to_all | solution.py:31
  220.4 1.9 collective-permute-start.1
  222.3 13.8 %collective-permute-done.1 = bf16[128,1024]{0,1:T(8,128)(2,1)S(1)} collective-permute-done((bf16[128,1024]{0,1:T(8,128)(2,1)S(1)}, bf16[128,1024]{0,1:T(8,128)(2,1)S(1)}, u32[]{:S(2)}, u32[]{:S(2)}) %collective-permute-start.1) | collective-permute-done | bytes 262176 | tf_op jit(solution)/shard_map/ppermute | solution.py:14
  236.9 11.8 %all-to-all-done.4 = bf16[64,2,16,256]{3,2,1,0:T(8,128)(2,1)S(1)} async-done(((bf16[64,2,16,256]{3,2,1,0:T(8,128)(2,1)}), bf16[64,2,16,256]{3,2,1,0:T(8,128)(2,1)S(1)}, u32[]{:S(2)}, u32[]{:S(2)}) %all-to-all-start.4) | async-done | bytes 1048608 | tf_op jit(solution)/shard_map/all_to_all | solution.py:31
  248.7 1.6 copy_convert_fusion
  (85 shorter events, 29.4 us)
Async XLA Ops:
  0.6 3.4 %copy-start = (bf16[2,1,1024,256]{3,2,1,0:T(8,128)(2,1)S(1)}, bf16[2,1,1024,256]{3,2,1,0:T(8,128)(2,1)}, u32[]{:S(2)}) copy-start(bf16[2,1,1024,256]{3,2,1,0:T(8,128)(2,1)} %param.6) | copy-start | bytes 3145732
  5.6 39.3 %all-to-all-start = ((bf16[16,128,256]{2,1,0:T(8,128)(2,1)}), bf16[16,128,256]{2,1,0:T(8,128)(2,1)}, u32[]{:S(2)}, u32[]{:S(2)}) async-start(bf16[16,128,256]{2,1,0:T(8,128)(2,1)} %broadcast_in_dim.118), calls=%async_computation | async-start | bytes 2097152 | tf_op jit(solution)/shard_map/all_to_all | solution.py:31
  21.1 26.6 %copy-start.7 = (pred[128,2048]{0,1:T(8,128)(4,1)}, pred[128,2048]{0,1:T(8,128)(4,1)S(1)}, u32[]{:S(2)}) copy-start(pred[128,2048]{0,1:T(8,128)(4,1)S(1)} %broadcast_compare_fusion.1) | copy-start | bytes 786436
  21.4 29.4 %copy-start.1 = (pred[2048,128]{1,0:T(8,128)(4,1)}, pred[2048,128]{1,0:T(8,128)(4,1)S(1)}, u32[]{:S(2)}) copy-start(pred[2048,128]{1,0:T(8,128)(4,1)S(1)} %broadcast_compare_fusion) | copy-start | bytes 786436
  53.5 8.7 %collective-permute-start = (bf16[128,1024]{0,1:T(8,128)(2,1)S(1)}, bf16[128,1024]{0,1:T(8,128)(2,1)S(1)}, u32[]{:S(2)}, u32[]{:S(2)}) collective-permute-start(bf16[128,1024]{0,1:T(8,128)(2,1)S(1)} %get-tuple-element.21), channel_id=1, source_target_pairs={{448,0},{0,64},{64,128},{128,192},{192,256},{256,320},{320,384},{3... | collective-permute-start | bytes 786440 | tf_op jit(solution)/shard_map/ppermute | solution.py:14
  62.6 0.7 copy-start.3
  65.3 57.4 %all-to-all-start.1 = ((bf16[16,256,256]{1,2,0:T(8,128)(2,1)}), bf16[16,256,256]{1,2,0:T(8,128)(2,1)S(1)}, u32[]{:S(2)}, u32[]{:S(2)}) async-start(bf16[16,256,256]{1,2,0:T(8,128)(2,1)} %maximum_maximum_fusion), calls=%async_computation.1 | async-start | bytes 4194304 | tf_op jit(solution)/shard_map/all_to_all | solution.py:31
  126.2 2.9 %copy-start.2 = (pred[2048,128]{1,0:T(8,128)(4,1)S(1)}, pred[2048,128]{1,0:T(8,128)(4,1)}, u32[]{:S(2)}) copy-start(pred[2048,128]{1,0:T(8,128)(4,1)} %copy-done.1) | copy-start | bytes 786436
  129.1 1.9 copy-start.4
  129.1 1.9 copy-start.5
  129.1 1.9 copy-start.8
  140.0 31.4 %all-to-all-start.2 = ((bf16[16,128,256]{1,2,0:T(8,128)(2,1)}), bf16[16,128,256]{1,2,0:T(8,128)(2,1)}, u32[]{:S(2)}, u32[]{:S(2)}) async-start(bf16[16,128,256]{1,2,0:T(8,128)(2,1)} %pad_maximum_fusion), calls=%async_computation.2 | async-start | bytes 2097152 | tf_op jit(solution)/shard_map/all_to_all | solution.py:31
  145.0 75.2 %copy-start.6 = (f32[128,8,128]{2,0,1:T(8,128)S(1)}, f32[128,8,128]{2,0,1:T(8,128)}, u32[]{:S(2)}) copy-start(f32[128,8,128]{2,0,1:T(8,128)} %get-tuple-element.27) | copy-start | bytes 1572868
  213.7 35.0 %all-to-all-start.4 = ((bf16[64,2,16,256]{3,2,1,0:T(8,128)(2,1)}), bf16[64,2,16,256]{3,2,1,0:T(8,128)(2,1)S(1)}, u32[]{:S(2)}, u32[]{:S(2)}) async-start(bf16[64,2,16,256]{3,2,1,0:T(8,128)(2,1)} %broadcast_in_dim.133), calls=%async_computation.4 | async-start | bytes 2097152 | tf_op jit(solution)/shard_map/all_to_all | solution.py:31
  220.4 15.7 %collective-permute-start.1 = (bf16[128,1024]{0,1:T(8,128)(2,1)S(1)}, bf16[128,1024]{0,1:T(8,128)(2,1)S(1)}, u32[]{:S(2)}, u32[]{:S(2)}) collective-permute-start(bf16[128,1024]{0,1:T(8,128)(2,1)S(1)} %fusion.19), channel_id=1, source_target_pairs={{448,0},{0,64},{64,128},{128,192},{192,256},{256,320},{320,384},{3... | collective-permute-start | bytes 786440 | tf_op jit(solution)/shard_map/ppermute | solution.py:14

commit v2 on v1

v2 whole, which is shorter than its diff:
```python
import functools
import math

import jax
import jax.numpy as jnp
from jax import lax
from jax.experimental import pallas as pl
from jax.experimental.pallas import tpu as pltpu
from jax.sharding import PartitionSpec as P

EPS = 1e-05
KEY_CHUNK = 256
NT = (((1,), (1,)), ((), ()))
TN = (((0,), (0,)), ((), ()))


def from_behind(block, axis, distance):
    devices = range(lax.axis_size(axis))
    route = [((i - distance) % len(devices), i) for i in devices]
    return lax.ppermute(block, axis, route)


def swap(blocks, axes):
    return lax.all_to_all(blocks, axes, 0, 0, tiled=True)


def rms_scale(values):
    return lax.rsqrt(jnp.mean(values * values, axis=-1, keepdims=True) + EPS)


def local_call(kernel, scalar_count, operand_count, outs):
    return pl.pallas_call(
        kernel,
        out_shape=[jax.ShapeDtypeStruct(shape, kind) for shape, kind in outs],
        in_specs=[pl.BlockSpec(memory_space=pltpu.SMEM)] * scalar_count
        + [pl.BlockSpec(memory_space=pltpu.VMEM)] * operand_count,
        out_specs=[pl.BlockSpec(memory_space=pltpu.VMEM)] * len(outs),
        compiler_params=pltpu.CompilerParams(vmem_limit_bytes=24 * 1024 * 1024),
    )


def span_at(starts, tick):
    count = starts.shape[0]
    anchor = lax.rem(lax.axis_index("pipe") + (count - tick % count), count)
    return lax.rem(starts[anchor] + lax.div(anchor + tick, count), 2)


def project_kernel(
    tick, starts, x_ref, weight_ref, *refs
):
    terms_ref = refs[0] if len(refs) == 7 else None
    kept_ref, query_ref, normed_ref, unit_ref, scale_ref, out_ref = refs[-6:]
    tok_rows, feat_width = x_ref.shape
    head_dim = unit_ref.shape[1]
    kept_ref[...] = x_ref[...]
    widened = x_ref[...].astype(jnp.float32)
    total = jnp.zeros((tok_rows, 1), jnp.float32)
    for head in range(feat_width // head_dim):
        part = widened[:, head * head_dim : (head + 1) * head_dim]
        square_sum = jnp.sum(part * part, axis=-1, keepdims=True)
        total = total + square_sum
        query = part * lax.rsqrt(square_sum * (1.0 / head_dim) + EPS)
        query_ref[head * tok_rows : (head + 1) * tok_rows, :] = query.astype(jnp.bfloat16)
    normed = (widened * lax.rsqrt(total * (1.0 / feat_width) + EPS)).astype(jnp.bfloat16)
    normed_ref[...] = normed
    projected = jnp.dot(normed, weight_ref[span_at(starts, tick)], preferred_element_type=jnp.float32)
    key_raw = projected[:, :head_dim]
    key_scale = rms_scale(key_raw)
    key_unit = key_raw * key_scale
    unit_ref[...] = key_unit
    scale_ref[...] = key_scale
    keys = key_unit.astype(jnp.bfloat16)
    values = projected[:, head_dim:].astype(jnp.bfloat16)
    for index in range(out_ref.shape[0]):
        out_ref[index, :tok_rows, :head_dim] = keys
        out_ref[index, :tok_rows, head_dim:] = values
        if terms_ref is not None:
            out_ref[index, tok_rows:, :] = terms_ref[index]


def forward_kernel(order, x_ref, query_ref, rows_ref, updated_ref, exp_ref, att_ref, recip_ref):
    tok_rows, feat_width = x_ref.shape
    ctx_count, _, pair_dim = rows_ref.shape
    head_dim = pair_dim // 2
    head_count = feat_width // head_dim
    half_len = tok_rows * ctx_count // order.shape[0]
    halves = tok_rows // half_len
    queries = query_ref[...]
    factor = math.log2(math.e) / math.sqrt(head_dim)

    def positions(block, shape, axis):
        row = lax.broadcasted_iota(jnp.int32, shape, axis)
        result = order[block * halves] * half_len + row
        for half in range(1, halves):
            later = (order[block * halves + half] - half) * half_len + row
            result = jnp.where(row >= half * half_len, later, result)
        return result

    own = positions(lax.axis_index("ctx"), (1, tok_rows), 1)
    own = jnp.concatenate([own] * head_count, axis=1)
    sums = jnp.zeros((1, head_count * tok_rows), jnp.float32)
    total = jnp.zeros((head_dim, head_count * tok_rows), jnp.float32)
    blocks = KEY_CHUNK // tok_rows
    for chunk in range(ctx_count // blocks):
        first = chunk * blocks
        rows = rows_ref[first : first + blocks, :, :].reshape(KEY_CHUNK, pair_dim)
        scores = lax.dot_general(
            rows[:, :head_dim], queries, NT, preferred_element_type=jnp.float32
        )
        where = jnp.concatenate(
            [positions(first + block, (tok_rows, 1), 0) for block in range(blocks)], axis=0
        )
        exponent = jnp.where(where <= own, jnp.exp2(scores * factor), 0.0)
        sums = sums + jnp.sum(exponent, axis=0, keepdims=True)
        kept = exponent.astype(jnp.bfloat16)
        exp_ref[first * tok_rows : (first + blocks) * tok_rows, :] = kept
        total = total + lax.dot_general(
            rows[:, head_dim:], kept, TN, preferred_element_type=jnp.float32
        )
    recip = 1.0 / sums
    recip_ref[...] = recip
    attended = total * recip
    att_ref[...] = attended
    parts = [
        attended[:, head * tok_rows : (head + 1) * tok_rows].T for head in range(head_count)
    ]
    output = jnp.concatenate(parts, axis=1)
    updated_ref[...] = (x_ref[...].astype(jnp.float32) + output * rms_scale(output)).astype(
        jnp.bfloat16
    )


def backward_kernel(query_ref, rows_ref, exp_ref, att_ref, recip_ref, grad_ref, terms_ref):
    ctx_count, tok_rows, pair_dim = rows_ref.shape
    head_dim = pair_dim // 2
    head_count = grad_ref.shape[1] // head_dim
    queries = query_ref[...]
    grad = grad_ref[...].astype(jnp.float32)
    turned = jnp.concatenate(
        [grad[:, head * head_dim : (head + 1) * head_dim].T for head in range(head_count)], axis=1
    )
    turned = (turned * recip_ref[...]).astype(jnp.bfloat16)
    row_delta = jnp.sum(turned.astype(jnp.float32) * att_ref[...], axis=0, keepdims=True)
    score_scale = 1.0 / math.sqrt(head_dim)
    blocks = KEY_CHUNK // tok_rows
    for chunk in range(ctx_count // blocks):
        first = chunk * blocks
        rows = rows_ref[first : first + blocks, :, :].reshape(KEY_CHUNK, pair_dim)
        kept = exp_ref[first * tok_rows : (first + blocks) * tok_rows, :]
        prob_grad = jnp.dot(rows[:, head_dim:], turned, preferred_element_type=jnp.float32)
        score_grad = (kept.astype(jnp.float32) * (prob_grad - row_delta)).astype(jnp.bfloat16)
        key_grad = jnp.dot(score_grad, queries, preferred_element_type=jnp.float32) * score_scale
        value_grad = lax.dot_general(kept, turned, NT, preferred_element_type=jnp.float32)
        both = jnp.concatenate([key_grad, value_grad], axis=1).astype(jnp.bfloat16)
        terms_ref[first : first + blocks, :, :] = both.reshape(blocks, tok_rows, pair_dim)


def finish_kernel(starts, *refs):
    parts_ref = refs[-1]
    dp_count, ctx_count, span_count, part_rows, pair_dim = parts_ref.shape
    head_dim = pair_dim // 2
    results = []
    for tick in range((len(refs) - 1) // 4):
        received_ref, normed_ref, unit_ref, scale_ref = refs[4 * tick : 4 * tick + 4]
        tok_rows = unit_ref.shape[0]
        sums = jnp.zeros((tok_rows, pair_dim), jnp.float32)
        for index in range(received_ref.shape[0]):
            sums = sums + received_ref[index].astype(jnp.float32)
        key_delta = sums[:, :head_dim]
        key_unit = unit_ref[...]
        key_back = scale_ref[...] * (
            key_delta - key_unit * jnp.mean(key_delta * key_unit, axis=-1, keepdims=True)
        )
        grad_rows = jnp.concatenate([key_back, sums[:, head_dim:]], axis=1).astype(jnp.bfloat16)
        results.append(
            lax.dot_general(normed_ref[...], grad_rows, TN, preferred_element_type=jnp.float32)
        )
    for span in range(span_count):
        value = jnp.zeros_like(results[0])
        for tick, result in enumerate(results):
            value = value + jnp.where(span_at(starts, tick) == span, result, 0.0)
        parts_ref[:, :, span] = value.astype(jnp.bfloat16).reshape(
            dp_count, ctx_count, part_rows, pair_dim
        )


def collect_kernel(parts_ref, out_ref):
    total = parts_ref[0].astype(jnp.float32)
    for index in range(1, parts_ref.shape[0]):
        total = total + parts_ref[index].astype(jnp.float32)
    summed = total.astype(jnp.bfloat16)
    for index in range(out_ref.shape[0]):
        out_ref[index] = summed


def collect(parts, copies):
    shape = (copies,) + parts.shape[1:]
    (result,) = local_call(collect_kernel, 0, 1, [(shape, jnp.bfloat16)])(parts)
    return result


def shards(state, weights, out_grad, start_span, block_order):
    tok_rows = state.shape[2]
    feat_width = state.shape[3]
    pair_dim = weights.shape[3]
    head_dim = pair_dim // 2
    head_count = feat_width // head_dim
    span_count = weights.shape[0]
    ctx_count = lax.axis_size("ctx")
    tick_count = out_grad.shape[0]
    starts = start_span[:, 0]
    half, wide = jnp.bfloat16, jnp.float32
    stacked = head_count * tok_rows
    seq_total = tok_rows * ctx_count
    carried = state[0, 0]
    layers = weights[:, 0]
    terms = None
    visits = []
    for tick_index in range(tick_count):
        extra = [] if terms is None else [terms]
        carried, queries, normed, key_unit, key_scale, outgoing = local_call(
            functools.partial(project_kernel, tick_index),
            1,
            2 + len(extra),
            [
                ((tok_rows, feat_width), half),
                ((stacked, head_dim), half),
                ((tok_rows, feat_width), half),
                ((tok_rows, head_dim), wide),
                ((tok_rows, 1), wide),
                ((ctx_count, tok_rows * (1 + len(extra)), pair_dim), half),
            ],
        )(starts, carried, layers, *extra)
        rows = swap(outgoing, "ctx")
        if visits:
            visits[-1][0] = rows[:, tok_rows:]
        rows = rows[:, :tok_rows]
        updated, exponents, attended, recip = local_call(
            forward_kernel,
            1,
            3,
            [
                ((tok_rows, feat_width), half),
                ((seq_total, stacked), half),
                ((head_dim, stacked), wide),
                ((1, stacked), wide),
            ],
        )(block_order, carried, queries, rows)
        carried = from_behind(updated, "pipe", 1)
        (terms,) = local_call(
            backward_kernel, 0, 6, [((ctx_count, tok_rows, pair_dim), half)]
        )(queries, rows, exponents, attended, recip, out_grad[tick_index, 0, 0])
        visits.append([None, normed, key_unit, key_scale])
    visits[-1][0] = swap(terms, "ctx")
    dp_count = lax.axis_size("dp")
    shape = (dp_count, ctx_count, span_count, feat_width // (dp_count * ctx_count), pair_dim)
    operands = [value for visit in visits for value in visit]
    (parts,) = local_call(finish_kernel, 1, len(operands), [(shape, half)])(starts, *operands)
    over_dp = collect(swap(parts, "dp"), 1)[0]
    over_ctx = swap(collect(swap(over_dp, "ctx"), ctx_count), "ctx")
    whole = swap(jnp.broadcast_to(over_ctx[None], (dp_count,) + over_ctx.shape), "dp")
    weight_grads = (
        whole.transpose(2, 0, 1, 3, 4)
        .reshape(span_count, feat_width, pair_dim)
        .astype(jnp.float32)
    )
    return (carried[None, None], weight_grads[:, None])


def solution(mesh):
    return jax.shard_map(
        shards,
        mesh=mesh,
        in_specs=(
            P("pipe", "dp", "ctx", None),
            P(None, "pipe", None, None),
            P(None, "pipe", "dp", "ctx", None),
            P(None, "dp"),
            P(),
        ),
        out_specs=(P("pipe", "dp", "ctx", None), P(None, "pipe", None, None)),
        check_vma=False,
    )
```

time: 251 us -> 224 us (0.89)
  the two profiles are of different devices: /device:TPU:16 before, /device:TPU:8 now
where the time goes in v2:
time: 224 us
  blocking collectives  171 us (76%)
  waiting for transfers between devices  19.5 us (9%)
  Pallas kernels  19.2 us (9%)
  starting transfers between devices  7.36 us (3%)
  local copies, waits for them, and re-layouts  4.8 us (2%)
    all_to_all x6, blocking collectives, swap(): return lax.all_to_all(blocks, axes, 0, 0, tiled=True)  171 us
    ppermute x2, waiting for transfers between devices, from_behind(): return lax.ppermute(block, axis, route)  17.5 us
    pallas_call x2, Pallas kernels, shards(): local_call(forward_kernel, 1, 3, [((tok_rows, feat_width), half), ((seq_t...  7.94 us
    pallas_call x2, Pallas kernels, shards(): local_call(backward_kernel, 0, 6, [((ctx_count, tok_rows, pair_dim), half)])  7.46 us
  transfers between devices with their start and end apart: 3, of which 3 were waited for; matrix products, arithmetic and copies ran while one was open for 0% of the time, Pallas kernels for 2%

profile of v2, /device:TPU:8, one launch (start us, length us, event | category | flops | bytes accessed | tf_op | source)
XLA Modules:
  0.0 223.9 jit_solution(11671100385186228280)
XLA Ops:
  0.7 1.2 copy-done
  1.9 0.9 copy-done.2
  3.5 1.1 shard_map.68
  4.6 39.5 %all_to_all.35.rows_ref = bf16[16,128,256]{2,1,0:T(8,128)(2,1)S(1)} all-to-all(bf16[16,128,256]{2,1,0:T(8,128)(2,1)S(1)} %get-tuple-element.24), channel_id=1, replica_groups=mesh['pipe'=8,'ctx'=16,'dp'=4] {'ctx'}, dimensions={0} | all-to-all | bytes 2097152 | tf_op jit(solution)/shard_map/all_to_all | solution.py:24
  44.1 4.0 %shard_map.69 = (bf16[128,1024]{1,0:T(8,128)(2,1)S(1)}, bf16[2048,1024]{1,0:T(8,128)(2,1)S(1)}, f32[128,1024]{1,0:T(8,128)S(1)}, f32[1,1024]{1,0:T(1,128)S(1)}) custom-call(s32[32]{0:T(128)S(1)} %copy-done.5, bf16[128,1024]{1,0:T(8,128)(2,1)S(1)} %get-tuple-element.22.x_ref, bf16[1024,128]{1,0:T(8,128)(2,1)S(1)} %get-tuple-element.23.query_ref, ...), custom_call_target="tpu_custom_call" | custom-call | tf_op jit(solution)/shard_map/pallas_call | solution.py:238
  48.1 1.9 collective-permute-start
  50.1 3.7 %shard_map.70.refs_0_ = bf16[16,128,256]{2,1,0:T(8,128)(2,1)S(1)} custom-call(bf16[1024,128]{1,0:T(8,128)(2,1)S(1)} %get-tuple-element.23.query_ref, bf16[16,128,256]{2,1,0:T(8,128)(2,1)S(1)} %all_to_all.35.rows_ref, bf16[2048,1024]{1,0:T(8,128)(2,1)S(1)} %get-tuple-element.26.exp_ref, f32[128,1024]{1,0:T(8,128)S(1)} %get-tuple-element.27.att_ref, ...), custom_call_target="tpu_custom_call" | custom-call | tf_op jit(solution)/shard_map/pallas_call | solution.py:250
  53.8 6.8 %collective-permute-done.x_ref = bf16[128,1024]{1,0:T(8,128)(2,1)S(1)} collective-permute-done((bf16[128,1024]{1,0:T(8,128)(2,1)S(1)}, bf16[128,1024]{1,0:T(8,128)(2,1)S(1)}, u32[]{:S(2)}, u32[]{:S(2)}) %collective-permute-start) | collective-permute-done | bytes 262176 | tf_op jit(solution)/shard_map/ppermute | solution.py:20
  60.6 1.2 shard_map.71
  61.8 53.3 %all_to_all.36 = bf16[16,256,256]{2,1,0:T(8,128)(2,1)S(1)} all-to-all(bf16[16,256,256]{2,1,0:T(8,128)(2,1)S(1)} %get-tuple-element.31), channel_id=1, replica_groups=mesh['pipe'=8,'ctx'=16,'dp'=4] {'ctx'}, dimensions={0} | all-to-all | bytes 4194304 | tf_op jit(solution)/shard_map/all_to_all | solution.py:24
  115.2 4.0 %shard_map.72 = (bf16[128,1024]{1,0:T(8,128)(2,1)S(1)}, bf16[2048,1024]{1,0:T(8,128)(2,1)S(1)}, f32[128,1024]{1,0:T(8,128)S(1)}, f32[1,1024]{1,0:T(1,128)S(1)}) custom-call(s32[32]{0:T(128)S(1)} %copy-done.5, bf16[128,1024]{1,0:T(8,128)(2,1)S(1)} %get-tuple-element.29.x_ref, bf16[1024,128]{1,0:T(8,128)(2,1)S(1)} %get-tuple-element.30.query_ref, ...), custom_call_target="tpu_custom_call" | custom-call | tf_op jit(solution)/shard_map/pallas_call | solution.py:238
  119.2 3.7 %shard_map.73 = bf16[16,128,256]{2,1,0:T(8,128)(2,1)S(1)} custom-call(bf16[1024,128]{1,0:T(8,128)(2,1)S(1)} %get-tuple-element.30.query_ref, bf16[16,128,256]{2,1,0:T(8,128)(2,1)S(1)} %get-tuple-element.45.rows_ref, bf16[2048,1024]{1,0:T(8,128)(2,1)S(1)} %get-tuple-element.36.exp_ref, f32[128,1024]{1,0:T(8,128)S(1)} %get-tuple-element.37.att_ref, ...), custom_call_target="tpu_custom_call" | custom-call | tf_op jit(solution)/shard_map/pallas_call | solution.py:250
  123.0 31.5 %all_to_all.37.refs_4_ = bf16[16,128,256]{2,1,0:T(8,128)(2,1)S(1)} all-to-all(bf16[16,128,256]{2,1,0:T(8,128)(2,1)S(1)} %shard_map.73), channel_id=1, replica_groups=mesh['pipe'=8,'ctx'=16,'dp'=4] {'ctx'}, dimensions={0} | all-to-all | bytes 2097152 | tf_op jit(solution)/shard_map/all_to_all | solution.py:24
  154.4 1.4 shard_map.74
  155.8 18.1 %all_to_all.38.parts_ref = bf16[4,16,2,16,256]{4,3,2,1,0:T(8,128)(2,1)S(1)} all-to-all(bf16[4,16,2,16,256]{4,3,2,1,0:T(8,128)(2,1)S(1)} %shard_map.74), channel_id=1, replica_groups=mesh['pipe'=8,'ctx'=16,'dp'=4] {'dp'}, dimensions={0} | all-to-all | bytes 2097152 | tf_op jit(solution)/shard_map/all_to_all | solution.py:24
  174.0 14.0 %all_to_all.39.parts_ref = bf16[16,2,16,256]{3,2,1,0:T(8,128)(2,1)S(1)} all-to-all(bf16[16,2,16,256]{3,2,1,0:T(8,128)(2,1)S(1)} %bitcast.16), channel_id=1, replica_groups=mesh['pipe'=8,'ctx'=16,'dp'=4] {'ctx'}, dimensions={0} | all-to-all | bytes 524288 | tf_op jit(solution)/shard_map/all_to_all | solution.py:24
  188.1 14.3 %all_to_all.40 = bf16[16,2,16,256]{3,2,1,0:T(8,128)(2,1)S(1)} all-to-all(bf16[16,2,16,256]{3,2,1,0:T(8,128)(2,1)S(1)} %shard_map.76), channel_id=1, replica_groups=mesh['pipe'=8,'ctx'=16,'dp'=4] {'ctx'}, dimensions={0} | all-to-all | bytes 524288 | tf_op jit(solution)/shard_map/all_to_all | solution.py:24
  202.3 1.1 broadcast_in_dim.5
  203.4 3.5 %all-to-all-start.6 = ((bf16[4,16,2,16,256]{4,3,1,2,0:T(8,128)(2,1)}), bf16[4,16,2,16,256]{4,3,1,2,0:T(8,128)(2,1)S(1)}, u32[]{:S(2)}, u32[]{:S(2)}) async-start(bf16[4,16,2,16,256]{4,3,1,2,0:T(8,128)(2,1)} %broadcast_in_dim.5), calls=%async_computation.6 | async-start | bytes 2097152 | tf_op jit(solution)/shard_map/all_to_all | solution.py:24
  206.9 1.9 collective-permute-start.1
  208.9 10.7 %collective-permute-done.1 = bf16[128,1024]{1,0:T(8,128)(2,1)S(1)} collective-permute-done((bf16[128,1024]{1,0:T(8,128)(2,1)S(1)}, bf16[128,1024]{1,0:T(8,128)(2,1)S(1)}, u32[]{:S(2)}, u32[]{:S(2)}) %collective-permute-start.1) | collective-permute-done | bytes 262176 | tf_op jit(solution)/shard_map/ppermute | solution.py:20
  219.5 2.0 all-to-all-done.6
  221.6 1.6 copy_convert_fusion
  223.2 0.7 copy.14
  (17 shorter events, 1.0 us)
Async XLA Ops:
  0.6 43.5 %copy-start.5 = (s32[32]{0:T(128)S(1)}, s32[32]{0:T(128)}, u32[]{:S(2)}) copy-start(s32[32]{0:T(128)} %order.3) | copy-start | bytes 388
  0.6 1.2 copy-start
  1.9 0.9 copy-start.2
  2.8 0.7 copy-start.3
  4.6 45.4 %copy-start.6 = (bf16[2,1,1,128,1024]{4,3,2,1,0:T(8,128)(2,1)S(1)}, bf16[2,1,1,128,1024]{4,3,2,1,0:T(8,128)(2,1)}, u32[]{:S(2)}) copy-start(bf16[2,1,1,128,1024]{4,3,2,1,0:T(8,128)(2,1)} %param.7) | copy-start | bytes 1572868
  48.1 12.5 %collective-permute-start = (bf16[128,1024]{1,0:T(8,128)(2,1)S(1)}, bf16[128,1024]{1,0:T(8,128)(2,1)S(1)}, u32[]{:S(2)}, u32[]{:S(2)}) collective-permute-start(bf16[128,1024]{1,0:T(8,128)(2,1)S(1)} %get-tuple-element.25), channel_id=1, source_target_pairs={{448,0},{0,64},{64,128},{128,192},{192,256},{256,320},{320,384},{3... | collective-permute-start | bytes 786440 | tf_op jit(solution)/shard_map/ppermute | solution.py:20
  50.1 10.5 %copy-start.1 = (bf16[2,1,1024,256]{3,2,1,0:T(8,128)(2,1)S(1)}, bf16[2,1,1024,256]{3,2,1,0:T(8,128)(2,1)}, u32[]{:S(2)}) copy-start(bf16[2,1,1024,256]{3,2,1,0:T(8,128)(2,1)} %param.6) | copy-start | bytes 3145732
  50.1 10.5 %copy-start.4 = (s32[8,1]{0,1:T(1,128)S(1)}, s32[8,1]{0,1:T(1,128)}, u32[]{:S(2)}) copy-start(s32[8,1]{0,1:T(1,128)} %param.8) | copy-start | bytes 100
  203.4 18.2 %all-to-all-start.6 = ((bf16[4,16,2,16,256]{4,3,1,2,0:T(8,128)(2,1)}), bf16[4,16,2,16,256]{4,3,1,2,0:T(8,128)(2,1)S(1)}, u32[]{:S(2)}, u32[]{:S(2)}) async-start(bf16[4,16,2,16,256]{4,3,1,2,0:T(8,128)(2,1)} %broadcast_in_dim.5), calls=%async_computation.6 | async-start | bytes 2097152 | tf_op jit(solution)/shard_map/all_to_all | solution.py:24
  206.9 12.6 %collective-permute-start.1 = (bf16[128,1024]{1,0:T(8,128)(2,1)S(1)}, bf16[128,1024]{1,0:T(8,128)(2,1)S(1)}, u32[]{:S(2)}, u32[]{:S(2)}) collective-permute-start(bf16[128,1024]{1,0:T(8,128)(2,1)S(1)} %get-tuple-element.32), channel_id=1, source_target_pairs={{448,0},{0,64},{64,128},{128,192},{192,256},{256,320},{320,384},{3... | collective-permute-start | bytes 786440 | tf_op jit(solution)/shard_map/ppermute | solution.py:20

commit v3 on v2

--- a/solution.py
+++ b/solution.py
@@ -9,7 +9,7 @@
 from jax.sharding import PartitionSpec as P
 
 EPS = 1e-05
-KEY_CHUNK = 256
+KEY_CHUNK = 512
 NT = (((1,), (1,)), ((), ()))
 TN = (((0,), (0,)), ((), ()))
 

time: 224 us -> 223 us (level)
  no operation moved by 1% of the time
where the time goes in v3:
time: 223 us
  blocking collectives  171 us (77%)
  waiting for transfers between devices  19.5 us (9%)
  Pallas kernels  18.1 us (8%)
  starting transfers between devices  7.36 us (3%)
  local copies, waits for them, and re-layouts  4.8 us (2%)
    all_to_all x6, blocking collectives, swap(): return lax.all_to_all(blocks, axes, 0, 0, tiled=True)  171 us
    ppermute x2, waiting for transfers between devices, from_behind(): return lax.ppermute(block, axis, route)  17.4 us
    pallas_call x2, Pallas kernels, shards(): local_call(backward_kernel, 0, 6, [((ctx_count, tok_rows, pair_dim), half)])  7.48 us
    pallas_call x2, Pallas kernels, shards(): local_call(forward_kernel, 1, 3, [((tok_rows, feat_width), half), ((seq_t...  6.83 us
  transfers between devices with their start and end apart: 3, of which 3 were waited for; matrix products, arithmetic and copies ran while one was open for 0% of the time, Pallas kernels for 2%

profile of v3, /device:TPU:8, one launch (start us, length us, event | category | flops | bytes accessed | tf_op | source)
XLA Modules:
  0.0 222.8 jit_solution(10986361362584800063)
XLA Ops:
  0.7 1.2 copy-done
  1.9 0.9 copy-done.2
  3.5 1.1 shard_map.68
  4.6 39.5 %all_to_all.35.rows_ref = bf16[16,128,256]{2,1,0:T(8,128)(2,1)S(1)} all-to-all(bf16[16,128,256]{2,1,0:T(8,128)(2,1)S(1)} %get-tuple-element.24), channel_id=1, replica_groups=mesh['pipe'=8,'ctx'=16,'dp'=4] {'ctx'}, dimensions={0} | all-to-all | bytes 2097152 | tf_op jit(solution)/shard_map/all_to_all | solution.py:24
  44.1 3.4 %shard_map.69 = (bf16[128,1024]{1,0:T(8,128)(2,1)S(1)}, bf16[2048,1024]{1,0:T(8,128)(2,1)S(1)}, f32[128,1024]{1,0:T(8,128)S(1)}, f32[1,1024]{1,0:T(1,128)S(1)}) custom-call(s32[32]{0:T(128)S(1)} %copy-done.5, bf16[128,1024]{1,0:T(8,128)(2,1)S(1)} %get-tuple-element.22.x_ref, bf16[1024,128]{1,0:T(8,128)(2,1)S(1)} %get-tuple-element.23.query_ref, ...), custom_call_target="tpu_custom_call" | custom-call | tf_op jit(solution)/shard_map/pallas_call | solution.py:238
  47.5 1.9 collective-permute-start
  49.5 3.7 %shard_map.70.refs_0_ = bf16[16,128,256]{2,1,0:T(8,128)(2,1)S(1)} custom-call(bf16[1024,128]{1,0:T(8,128)(2,1)S(1)} %get-tuple-element.23.query_ref, bf16[16,128,256]{2,1,0:T(8,128)(2,1)S(1)} %all_to_all.35.rows_ref, bf16[2048,1024]{1,0:T(8,128)(2,1)S(1)} %get-tuple-element.26.exp_ref, f32[128,1024]{1,0:T(8,128)S(1)} %get-tuple-element.27.att_ref, ...), custom_call_target="tpu_custom_call" | custom-call | tf_op jit(solution)/shard_map/pallas_call | solution.py:250
  53.3 6.8 %collective-permute-done.x_ref = bf16[128,1024]{1,0:T(8,128)(2,1)S(1)} collective-permute-done((bf16[128,1024]{1,0:T(8,128)(2,1)S(1)}, bf16[128,1024]{1,0:T(8,128)(2,1)S(1)}, u32[]{:S(2)}, u32[]{:S(2)}) %collective-permute-start) | collective-permute-done | bytes 262176 | tf_op jit(solution)/shard_map/ppermute | solution.py:20
  60.0 1.2 shard_map.71
  61.2 52.8 %all_to_all.36 = bf16[16,256,256]{2,1,0:T(8,128)(2,1)S(1)} all-to-all(bf16[16,256,256]{2,1,0:T(8,128)(2,1)S(1)} %get-tuple-element.31), channel_id=1, replica_groups=mesh['pipe'=8,'ctx'=16,'dp'=4] {'ctx'}, dimensions={0} | all-to-all | bytes 4194304 | tf_op jit(solution)/shard_map/all_to_all | solution.py:24
  114.2 3.4 %shard_map.72 = (bf16[128,1024]{1,0:T(8,128)(2,1)S(1)}, bf16[2048,1024]{1,0:T(8,128)(2,1)S(1)}, f32[128,1024]{1,0:T(8,128)S(1)}, f32[1,1024]{1,0:T(1,128)S(1)}) custom-call(s32[32]{0:T(128)S(1)} %copy-done.5, bf16[128,1024]{1,0:T(8,128)(2,1)S(1)} %get-tuple-element.29.x_ref, bf16[1024,128]{1,0:T(8,128)(2,1)S(1)} %get-tuple-element.30.query_ref, ...), custom_call_target="tpu_custom_call" | custom-call | tf_op jit(solution)/shard_map/pallas_call | solution.py:238
  117.6 3.7 %shard_map.73 = bf16[16,128,256]{2,1,0:T(8,128)(2,1)S(1)} custom-call(bf16[1024,128]{1,0:T(8,128)(2,1)S(1)} %get-tuple-element.30.query_ref, bf16[16,128,256]{2,1,0:T(8,128)(2,1)S(1)} %get-tuple-element.45.rows_ref, bf16[2048,1024]{1,0:T(8,128)(2,1)S(1)} %get-tuple-element.36.exp_ref, f32[128,1024]{1,0:T(8,128)S(1)} %get-tuple-element.37.att_ref, ...), custom_call_target="tpu_custom_call" | custom-call | tf_op jit(solution)/shard_map/pallas_call | solution.py:250
  121.3 31.1 %all_to_all.37.refs_4_ = bf16[16,128,256]{2,1,0:T(8,128)(2,1)S(1)} all-to-all(bf16[16,128,256]{2,1,0:T(8,128)(2,1)S(1)} %shard_map.73), channel_id=1, replica_groups=mesh['pipe'=8,'ctx'=16,'dp'=4] {'ctx'}, dimensions={0} | all-to-all | bytes 2097152 | tf_op jit(solution)/shard_map/all_to_all | solution.py:24
  152.5 1.4 shard_map.74
  153.9 19.0 %all_to_all.38.parts_ref = bf16[4,16,2,16,256]{4,3,2,1,0:T(8,128)(2,1)S(1)} all-to-all(bf16[4,16,2,16,256]{4,3,2,1,0:T(8,128)(2,1)S(1)} %shard_map.74), channel_id=1, replica_groups=mesh['pipe'=8,'ctx'=16,'dp'=4] {'dp'}, dimensions={0} | all-to-all | bytes 2097152 | tf_op jit(solution)/shard_map/all_to_all | solution.py:24
  173.0 13.9 %all_to_all.39.parts_ref = bf16[16,2,16,256]{3,2,1,0:T(8,128)(2,1)S(1)} all-to-all(bf16[16,2,16,256]{3,2,1,0:T(8,128)(2,1)S(1)} %bitcast.16), channel_id=1, replica_groups=mesh['pipe'=8,'ctx'=16,'dp'=4] {'ctx'}, dimensions={0} | all-to-all | bytes 524288 | tf_op jit(solution)/shard_map/all_to_all | solution.py:24
  187.0 14.2 %all_to_all.40 = bf16[16,2,16,256]{3,2,1,0:T(8,128)(2,1)S(1)} all-to-all(bf16[16,2,16,256]{3,2,1,0:T(8,128)(2,1)S(1)} %shard_map.76), channel_id=1, replica_groups=mesh['pipe'=8,'ctx'=16,'dp'=4] {'ctx'}, dimensions={0} | all-to-all | bytes 524288 | tf_op jit(solution)/shard_map/all_to_all | solution.py:24
  201.2 1.1 broadcast_in_dim.5
  202.3 3.5 %all-to-all-start.6 = ((bf16[4,16,2,16,256]{4,3,1,2,0:T(8,128)(2,1)}), bf16[4,16,2,16,256]{4,3,1,2,0:T(8,128)(2,1)S(1)}, u32[]{:S(2)}, u32[]{:S(2)}) async-start(bf16[4,16,2,16,256]{4,3,1,2,0:T(8,128)(2,1)} %broadcast_in_dim.5), calls=%async_computation.6 | async-start | bytes 2097152 | tf_op jit(solution)/shard_map/all_to_all | solution.py:24
  205.8 1.9 collective-permute-start.1
  207.7 10.7 %collective-permute-done.1 = bf16[128,1024]{1,0:T(8,128)(2,1)S(1)} collective-permute-done((bf16[128,1024]{1,0:T(8,128)(2,1)S(1)}, bf16[128,1024]{1,0:T(8,128)(2,1)S(1)}, u32[]{:S(2)}, u32[]{:S(2)}) %collective-permute-start.1) | collective-permute-done | bytes 262176 | tf_op jit(solution)/shard_map/ppermute | solution.py:20
  218.4 2.1 all-to-all-done.6
  220.5 1.6 copy_convert_fusion
  222.1 0.7 copy.14
  (17 shorter events, 1.0 us)
Async XLA Ops:
  0.6 43.5 %copy-start.5 = (s32[32]{0:T(128)S(1)}, s32[32]{0:T(128)}, u32[]{:S(2)}) copy-start(s32[32]{0:T(128)} %order.3) | copy-start | bytes 388
  0.6 1.2 copy-start
  1.9 0.9 copy-start.2
  2.8 0.7 copy-start.3
  4.6 44.9 %copy-start.6 = (bf16[2,1,1,128,1024]{4,3,2,1,0:T(8,128)(2,1)S(1)}, bf16[2,1,1,128,1024]{4,3,2,1,0:T(8,128)(2,1)}, u32[]{:S(2)}) copy-start(bf16[2,1,1,128,1024]{4,3,2,1,0:T(8,128)(2,1)} %param.7) | copy-start | bytes 1572868
  47.5 12.5 %collective-permute-start = (bf16[128,1024]{1,0:T(8,128)(2,1)S(1)}, bf16[128,1024]{1,0:T(8,128)(2,1)S(1)}, u32[]{:S(2)}, u32[]{:S(2)}) collective-permute-start(bf16[128,1024]{1,0:T(8,128)(2,1)S(1)} %get-tuple-element.25), channel_id=1, source_target_pairs={{448,0},{0,64},{64,128},{128,192},{192,256},{256,320},{320,384},{3... | collective-permute-start | bytes 786440 | tf_op jit(solution)/shard_map/ppermute | solution.py:20
  49.5 10.5 %copy-start.1 = (bf16[2,1,1024,256]{3,2,1,0:T(8,128)(2,1)S(1)}, bf16[2,1,1024,256]{3,2,1,0:T(8,128)(2,1)}, u32[]{:S(2)}) copy-start(bf16[2,1,1024,256]{3,2,1,0:T(8,128)(2,1)} %param.6) | copy-start | bytes 3145732
  49.5 10.5 %copy-start.4 = (s32[8,1]{0,1:T(1,128)S(1)}, s32[8,1]{0,1:T(1,128)}, u32[]{:S(2)}) copy-start(s32[8,1]{0,1:T(1,128)} %param.8) | copy-start | bytes 100
  202.3 18.2 %all-to-all-start.6 = ((bf16[4,16,2,16,256]{4,3,1,2,0:T(8,128)(2,1)}), bf16[4,16,2,16,256]{4,3,1,2,0:T(8,128)(2,1)S(1)}, u32[]{:S(2)}, u32[]{:S(2)}) async-start(bf16[4,16,2,16,256]{4,3,1,2,0:T(8,128)(2,1)} %broadcast_in_dim.5), calls=%async_computation.6 | async-start | bytes 2097152 | tf_op jit(solution)/shard_map/all_to_all | solution.py:24
  205.8 12.6 %collective-permute-start.1 = (bf16[128,1024]{1,0:T(8,128)(2,1)S(1)}, bf16[128,1024]{1,0:T(8,128)(2,1)S(1)}, u32[]{:S(2)}, u32[]{:S(2)}) collective-permute-start(bf16[128,1024]{1,0:T(8,128)(2,1)S(1)} %get-tuple-element.32), channel_id=1, source_target_pairs={{448,0},{0,64},{64,128},{128,192},{192,256},{256,320},{320,384},{3... | collective-permute-start | bytes 786440 | tf_op jit(solution)/shard_map/ppermute | solution.py:20

commit v4 on v3

--- a/solution.py
+++ b/solution.py
@@ -251,14 +251,16 @@
             backward_kernel, 0, 6, [((ctx_count, tok_rows, pair_dim), half)]
         )(queries, rows, exponents, attended, recip, out_grad[tick_index, 0, 0])
         visits.append([None, normed, key_unit, key_scale])
-    visits[-1][0] = swap(terms, "ctx")
+    received, carried = lax.optimization_barrier((swap(terms, "ctx"), carried))
+    visits[-1][0] = received
     dp_count = lax.axis_size("dp")
     shape = (dp_count, ctx_count, span_count, feat_width // (dp_count * ctx_count), pair_dim)
     operands = [value for visit in visits for value in visit]
     (parts,) = local_call(finish_kernel, 1, len(operands), [(shape, half)])(starts, *operands)
     over_dp = collect(swap(parts, "dp"), 1)[0]
     over_ctx = swap(collect(swap(over_dp, "ctx"), ctx_count), "ctx")
-    whole = swap(jnp.broadcast_to(over_ctx[None], (dp_count,) + over_ctx.shape), "dp")
+    copies = jnp.broadcast_to(over_ctx[None], (dp_count,) + over_ctx.shape)
+    whole, carried = lax.optimization_barrier((swap(copies, "dp"), carried))
     weight_grads = (
         whole.transpose(2, 0, 1, 3, 4)
         .reshape(span_count, feat_width, pair_dim)

time: 223 us -> 223 us (level)
  blocking collectives: 171 us -> 157 us
  waiting for transfers between devices: 19.5 us -> 30.5 us
    all_to_all x6, blocking collectives: 171 us -> 157 us  [swap(): return lax.all_to_all(blocks, axes, 0, 0, tiled=True)]
    all_to_all x1, waiting for transfers between devices: 2.1 us -> 15.8 us  [swap(): return lax.all_to_all(blocks, axes, 0, 0, tiled=True)]
    ppermute x2, waiting for transfers between devices: 17.4 us -> 14.7 us  [from_behind(): return lax.ppermute(block, axis, route)]
where the time goes in v4:
time: 223 us; the launch traced here: 222 us
  blocking collectives  157 us (70%)
  waiting for transfers between devices  30.5 us (14%)
  Pallas kernels  19 us (9%)
  starting transfers between devices  9.39 us (4%)
  local copies, waits for them, and re-layouts  3.83 us (2%)
    all_to_all x6, blocking collectives, swap(): return lax.all_to_all(blocks, axes, 0, 0, tiled=True)  157 us
    all_to_all x1, waiting for transfers between devices, swap(): return lax.all_to_all(blocks, axes, 0, 0, tiled=True)  15.8 us
    ppermute x2, waiting for transfers between devices, from_behind(): return lax.ppermute(block, axis, route)  14.7 us
    pallas_call x2, Pallas kernels, shards(): local_call(backward_kernel, 0, 6, [((ctx_count, tok_rows, pair_dim), half)])  8.45 us
    pallas_call x2, Pallas kernels, shards(): local_call(forward_kernel, 1, 3, [((tok_rows, feat_width), half), ((seq_t...  6.81 us
    all_to_all x1, starting transfers between devices, swap(): return lax.all_to_all(blocks, axes, 0, 0, tiled=True)  5.57 us
  transfers between devices with their start and end apart: 3, of which 3 were waited for; matrix products, arithmetic and copies ran while one was open for 0% of the time, Pallas kernels for 2%

profile of v4, /device:TPU:8, one launch (start us, length us, event | category | flops | bytes accessed | tf_op | source)
XLA Modules:
  0.0 222.1 jit_solution(4307242230817872001)
XLA Ops:
  0.7 1.2 copy-done
  1.9 0.9 copy-done.2
  2.8 0.7 copy-done.3
  3.5 1.1 shard_map.68
  4.6 39.5 %all_to_all.35.rows_ref = bf16[16,128,256]{2,1,0:T(8,128)(2,1)S(1)} all-to-all(bf16[16,128,256]{2,1,0:T(8,128)(2,1)S(1)} %get-tuple-element.28), channel_id=1, replica_groups=mesh['pipe'=8,'ctx'=16,'dp'=4] {'ctx'}, dimensions={0} | all-to-all | bytes 2097152 | tf_op jit(solution)/shard_map/all_to_all | solution.py:24
  44.1 3.4 %shard_map.69 = (bf16[128,1024]{1,0:T(8,128)(2,1)S(1)}, bf16[2048,1024]{1,0:T(8,128)(2,1)S(1)}, f32[128,1024]{1,0:T(8,128)S(1)}, f32[1,1024]{1,0:T(1,128)S(1)}) custom-call(s32[32]{0:T(128)S(1)} %copy-done.5, bf16[128,1024]{1,0:T(8,128)(2,1)S(1)} %get-tuple-element.26.x_ref, bf16[1024,128]{1,0:T(8,128)(2,1)S(1)} %get-tuple-element.27.query_ref, ...), custom_call_target="tpu_custom_call" | custom-call | tf_op jit(solution)/shard_map/pallas_call | solution.py:238
  47.5 1.9 collective-permute-start
  49.5 3.7 %shard_map.70.refs_0_ = bf16[16,128,256]{2,1,0:T(8,128)(2,1)S(1)} custom-call(bf16[1024,128]{1,0:T(8,128)(2,1)S(1)} %get-tuple-element.27.query_ref, bf16[16,128,256]{2,1,0:T(8,128)(2,1)S(1)} %all_to_all.35.rows_ref, bf16[2048,1024]{1,0:T(8,128)(2,1)S(1)} %get-tuple-element.30.exp_ref, f32[128,1024]{1,0:T(8,128)S(1)} %get-tuple-element.31.att_ref, ...), custom_call_target="tpu_custom_call" | custom-call | tf_op jit(solution)/shard_map/pallas_call | solution.py:250
  53.3 6.8 %collective-permute-done.x_ref = bf16[128,1024]{1,0:T(8,128)(2,1)S(1)} collective-permute-done((bf16[128,1024]{1,0:T(8,128)(2,1)S(1)}, bf16[128,1024]{1,0:T(8,128)(2,1)S(1)}, u32[]{:S(2)}, u32[]{:S(2)}) %collective-permute-start) | collective-permute-done | bytes 262176 | tf_op jit(solution)/shard_map/ppermute | solution.py:20
  60.1 1.2 shard_map.71
  61.2 52.4 %all_to_all.36 = bf16[16,256,256]{2,1,0:T(8,128)(2,1)S(1)} all-to-all(bf16[16,256,256]{2,1,0:T(8,128)(2,1)S(1)} %get-tuple-element.33), channel_id=1, replica_groups=mesh['pipe'=8,'ctx'=16,'dp'=4] {'ctx'}, dimensions={0} | all-to-all | bytes 4194304 | tf_op jit(solution)/shard_map/all_to_all | solution.py:24
  113.7 3.4 %shard_map.72 = (bf16[128,1024]{1,0:T(8,128)(2,1)S(1)}, bf16[2048,1024]{1,0:T(8,128)(2,1)S(1)}, f32[128,1024]{1,0:T(8,128)S(1)}, f32[1,1024]{1,0:T(1,128)S(1)}) custom-call(s32[32]{0:T(128)S(1)} %copy-done.5, bf16[128,1024]{1,0:T(8,128)(2,1)S(1)} %get-tuple-element.38.x_ref, bf16[1024,128]{1,0:T(8,128)(2,1)S(1)} %get-tuple-element.37.query_ref, ...), custom_call_target="tpu_custom_call" | custom-call | tf_op jit(solution)/shard_map/pallas_call | solution.py:238
  117.2 4.7 %shard_map.73 = bf16[16,128,256]{2,1,0:T(8,128)(2,1)} custom-call(bf16[1024,128]{1,0:T(8,128)(2,1)S(1)} %get-tuple-element.37.query_ref, bf16[16,128,256]{2,1,0:T(8,128)(2,1)S(1)} %get-tuple-element.52.rows_ref, bf16[2048,1024]{1,0:T(8,128)(2,1)S(1)} %get-tuple-element.39.exp_ref, f32[128,1024]{1,0:T(8,128)S(1)} %get-tuple-element.40.att_ref, ...), custom_call_target="tpu_custom_call" | custom-call | tf_op jit(solution)/shard_map/pallas_call | solution.py:250
  121.9 5.6 %all-to-all-start.2 = ((bf16[16,128,256]{2,1,0:T(8,128)(2,1)}), bf16[16,128,256]{2,1,0:T(8,128)(2,1)S(1)}, u32[]{:S(2)}, u32[]{:S(2)}) async-start(bf16[16,128,256]{2,1,0:T(8,128)(2,1)} %shard_map.73), calls=%async_computation.2 | async-start | bytes 2097152 | tf_op jit(solution)/shard_map/all_to_all | solution.py:24
  127.4 1.9 collective-permute-start.1
  129.3 8.0 %collective-permute-done.1 = bf16[128,1024]{1,0:T(8,128)(2,1)S(1)} collective-permute-done((bf16[128,1024]{1,0:T(8,128)(2,1)S(1)}, bf16[128,1024]{1,0:T(8,128)(2,1)S(1)}, u32[]{:S(2)}, u32[]{:S(2)}) %collective-permute-start.1) | collective-permute-done | bytes 262176 | tf_op jit(solution)/shard_map/ppermute | solution.py:20
  137.3 15.8 %all-to-all-done.2.refs_4_ = bf16[16,128,256]{2,1,0:T(8,128)(2,1)S(1)} async-done(((bf16[16,128,256]{2,1,0:T(8,128)(2,1)}), bf16[16,128,256]{2,1,0:T(8,128)(2,1)S(1)}, u32[]{:S(2)}, u32[]{:S(2)}) %all-to-all-start.2) | async-done | bytes 1048608 | tf_op jit(solution)/shard_map/all_to_all | solution.py:24
  153.1 1.3 shard_map.74
  154.4 17.5 %all_to_all.37.parts_ref = bf16[4,16,2,16,256]{4,3,2,1,0:T(8,128)(2,1)S(1)} all-to-all(bf16[4,16,2,16,256]{4,3,2,1,0:T(8,128)(2,1)S(1)} %shard_map.74), channel_id=1, replica_groups=mesh['pipe'=8,'ctx'=16,'dp'=4] {'dp'}, dimensions={0} | all-to-all | bytes 2097152 | tf_op jit(solution)/shard_map/all_to_all | solution.py:24
  172.1 17.0 %all_to_all.38.parts_ref = bf16[16,2,16,256]{3,2,1,0:T(8,128)(2,1)S(1)} all-to-all(bf16[16,2,16,256]{3,2,1,0:T(8,128)(2,1)S(1)} %bitcast.16), channel_id=1, replica_groups=mesh['pipe'=8,'ctx'=16,'dp'=4] {'ctx'}, dimensions={0} | all-to-all | bytes 524288 | tf_op jit(solution)/shard_map/all_to_all | solution.py:24
  189.1 13.3 %all_to_all.39 = bf16[16,2,16,256]{3,2,1,0:T(8,128)(2,1)S(1)} all-to-all(bf16[16,2,16,256]{3,2,1,0:T(8,128)(2,1)S(1)} %shard_map.76), channel_id=1, replica_groups=mesh['pipe'=8,'ctx'=16,'dp'=4] {'ctx'}, dimensions={0} | all-to-all | bytes 524288 | tf_op jit(solution)/shard_map/all_to_all | solution.py:24
  202.5 17.3 %all_to_all.40 = bf16[4,16,2,16,256]{4,3,1,2,0:T(8,128)(2,1)S(1)} all-to-all(bf16[4,16,2,16,256]{4,3,1,2,0:T(8,128)(2,1)S(1)} %broadcast_in_dim.4), channel_id=1, replica_groups=mesh['pipe'=8,'ctx'=16,'dp'=4] {'dp'}, dimensions={0} | all-to-all | bytes 2097152 | tf_op jit(solution)/shard_map/all_to_all | solution.py:24
  219.8 1.6 copy_convert_fusion
  221.4 0.7 copy.14
  (17 shorter events, 0.5 us)
Async XLA Ops:
  0.6 43.5 %copy-start.5 = (s32[32]{0:T(128)S(1)}, s32[32]{0:T(128)}, u32[]{:S(2)}) copy-start(s32[32]{0:T(128)} %order.3) | copy-start | bytes 388
  0.6 1.2 copy-start
  1.9 0.9 copy-start.2
  2.8 0.7 copy-start.3
  4.6 44.9 %copy-start.6 = (bf16[2,1,1,128,1024]{4,3,2,1,0:T(8,128)(2,1)S(1)}, bf16[2,1,1,128,1024]{4,3,2,1,0:T(8,128)(2,1)}, u32[]{:S(2)}) copy-start(bf16[2,1,1,128,1024]{4,3,2,1,0:T(8,128)(2,1)} %param.7) | copy-start | bytes 1572868
  47.5 12.5 %collective-permute-start = (bf16[128,1024]{1,0:T(8,128)(2,1)S(1)}, bf16[128,1024]{1,0:T(8,128)(2,1)S(1)}, u32[]{:S(2)}, u32[]{:S(2)}) collective-permute-start(bf16[128,1024]{1,0:T(8,128)(2,1)S(1)} %get-tuple-element.29), channel_id=1, source_target_pairs={{448,0},{0,64},{64,128},{128,192},{192,256},{256,320},{320,384},{3... | collective-permute-start | bytes 786440 | tf_op jit(solution)/shard_map/ppermute | solution.py:20
  49.5 10.5 %copy-start.1 = (bf16[2,1,1024,256]{3,2,1,0:T(8,128)(2,1)S(1)}, bf16[2,1,1024,256]{3,2,1,0:T(8,128)(2,1)}, u32[]{:S(2)}) copy-start(bf16[2,1,1024,256]{3,2,1,0:T(8,128)(2,1)} %param.6) | copy-start | bytes 3145732
  49.5 10.5 %copy-start.4 = (s32[8,1]{0,1:T(1,128)S(1)}, s32[8,1]{0,1:T(1,128)}, u32[]{:S(2)}) copy-start(s32[8,1]{0,1:T(1,128)} %param.8) | copy-start | bytes 100
  121.9 31.2 %all-to-all-start.2 = ((bf16[16,128,256]{2,1,0:T(8,128)(2,1)}), bf16[16,128,256]{2,1,0:T(8,128)(2,1)S(1)}, u32[]{:S(2)}, u32[]{:S(2)}) async-start(bf16[16,128,256]{2,1,0:T(8,128)(2,1)} %shard_map.73), calls=%async_computation.2 | async-start | bytes 2097152 | tf_op jit(solution)/shard_map/all_to_all | solution.py:24
  127.4 9.9 %collective-permute-start.1 = (bf16[128,1024]{1,0:T(8,128)(2,1)S(1)}, bf16[128,1024]{1,0:T(8,128)(2,1)S(1)}, u32[]{:S(2)}, u32[]{:S(2)}) collective-permute-start(bf16[128,1024]{1,0:T(8,128)(2,1)S(1)} %get-tuple-element.42), channel_id=1, source_target_pairs={{448,0},{0,64},{64,128},{128,192},{192,256},{256,320},{320,384},{3... | collective-permute-start | bytes 786440 | tf_op jit(solution)/shard_map/ppermute | solution.py:20
